TPU v7x, 32 devices: a whole 2x2x4 slice. The times are simulated.
32 devices in a mesh: rows: 16 (over z, y, x), heads: 2 (over core).
Axes of the slice: x: 2, y: 2, z: 4, core: 2. Of those that a mesh axis runs over, the one named last changes fastest.
Arguments:
- tokens: bfloat16 [32768, 768], P(('rows', 'heads')), may hold values from -6 to 6
- cotangent: bfloat16 [32768, 768], P(('rows', 'heads')), may hold values from -6 to 6
- segment_ids: int32 [64, 512], P('rows'), may hold values from 0 to 7, never falling along the last dimension, each value on 1 to 256 neighbouring positions
- valid_count: int32 [64], P('rows'), may hold values from 1 to 512, 24576 in all
- qkv_weight: bfloat16 [768, 2304], P(('rows', 'heads')), may hold values from -0.21875 to 0.21875
- qv_bias: bfloat16 [2, 768], P(None, ('rows', 'heads')), may hold values from -0.59765625 to 0.59765625
- out_weight: bfloat16 [768, 768], P(('rows', 'heads')), may hold values from -1.75 to 1.75
- out_bias: bfloat16 [768], P(('rows', 'heads')), may hold values from -1.796875 to 1.796875
- norm_gain: bfloat16 [768], P(('rows', 'heads')), may hold values from 0.5 to 1.5
- norm_shift: bfloat16 [768], P(('rows', 'heads')), may hold values from -1.796875 to 1.796875
- in_weight: bfloat16 [768, 3072], P(('rows', 'heads')), may hold values from -0.21875 to 0.21875
- in_bias: bfloat16 [3072], P(('rows', 'heads')), may hold values from -1.796875 to 1.796875
- back_weight: bfloat16 [3072, 768], P(('rows', 'heads')), may hold values from -0.109375 to 0.109375
- back_bias: bfloat16 [768], P(('rows', 'heads')), may hold values from -1.796875 to 1.796875
- final_gain: bfloat16 [768], P(('rows', 'heads')), may hold values from 0.5 to 1.5
- final_shift: bfloat16 [768], P(('rows', 'heads')), may hold values from -1.796875 to 1.796875
Outputs:
- layer_out: bfloat16 [32768, 768], P(('rows', 'heads'))
- grad_tokens: float32 [32768, 768], P(('rows', 'heads'))
- grad_qkv_weight: float32 [768, 2304], P(('rows', 'heads'))
- grad_qv_bias: float32 [2, 768], P(None, ('rows', 'heads'))
- grad_out_weight: float32 [768, 768], P(('rows', 'heads'))
- grad_out_bias: float32 [768], P(('rows', 'heads'))
- grad_norm_gain: float32 [768], P(('rows', 'heads'))
- grad_norm_shift: float32 [768], P(('rows', 'heads'))
- grad_in_weight: float32 [768, 3072], P(('rows', 'heads'))
- grad_in_bias: float32 [3072], P(('rows', 'heads'))
- grad_back_weight: float32 [3072, 768], P(('rows', 'heads'))
- grad_back_bias: float32 [768], P(('rows', 'heads'))
- grad_final_gain: float32 [768], P(('rows', 'heads'))
- grad_final_shift: float32 [768], P(('rows', 'heads'))
Inputs may be any that keep to these rules, and one draw needn't show every extreme that they name: `segment_ids`: along a row the numbers never fall; each segment spans 1 to 256 positions. `valid_count`: the counts of all 64 rows sum to 24576.
All inputs are finite; a program needn't handle non-finite values. No bound on the sum of `valid_count` on one device may be relied on, other than what follows from the above.
Results may differ from a plain program's by a relative error of at most 0.013.
Values may be sent and summed in bfloat16 or wider, within the bound.
No kernel may reach another device: no remote copies, remote signals or barrier semaphores. Data moves between devices by JAX's collectives and lax.ppermute only.
A program may use at most 192 MiB of HBM per device.

v0:
```python
import math
import jax
import jax.numpy as jnp
from jax import lax
from jax.sharding import PartitionSpec as P

HEADS = 12
HEAD_DIM = 64
EPS = 1e-12
AXES = ("rows", "heads")
F32 = jnp.float32
BF16 = jnp.bfloat16


def norm_forward(values, gain_row, shift_row):
    centered = values - jnp.mean(values, axis=-1, keepdims=True)
    inverse = lax.rsqrt(jnp.mean(centered * centered, axis=-1, keepdims=True) + EPS)
    normalized = centered * inverse
    return (normalized * gain_row + shift_row, normalized, inverse)


def norm_backward(grad_output, normalized, inverse, gain_row):
    grad_normed = grad_output * gain_row
    grad_input = inverse * (
        grad_normed
        - jnp.mean(grad_normed, axis=-1, keepdims=True)
        - normalized * jnp.mean(grad_normed * normalized, axis=-1, keepdims=True)
    )
    return (grad_input, jnp.sum(grad_output * normalized, axis=0), jnp.sum(grad_output, axis=0))


def allowed_keys(segment_row, count_row):
    positions = jnp.arange(segment_row.shape[0])
    same_segment = segment_row[:, None] == segment_row[None, :]
    return same_segment & (positions[None, :] < count_row) | (
        positions[:, None] == positions[None, :]
    )


def masked_scores(query_rows, key_rows, allowed):
    scores = jnp.einsum(
        "qhd,khd->hqk", query_rows, key_rows, preferred_element_type=F32
    ) * HEAD_DIM ** (-0.5)
    return jnp.where(allowed[None], scores, -1e30)


def attend_forward(query_rows, key_rows, value_rows, segment_row, count_row):
    scores = masked_scores(query_rows, key_rows, allowed_keys(segment_row, count_row))
    highest = jnp.max(scores, axis=-1, keepdims=True)
    exponent = jnp.exp(scores - highest)
    total = jnp.sum(exponent, axis=-1, keepdims=True)
    low = (exponent / total).astype(BF16)
    context = jnp.einsum("hqk,khd->qhd", low, value_rows, preferred_element_type=F32)
    return (context.astype(BF16), (highest + jnp.log(total))[..., 0])


def attend_backward(query_rows, key_rows, value_rows, segment_row, count_row, lse, grad_context):
    scores = masked_scores(query_rows, key_rows, allowed_keys(segment_row, count_row))
    soft = jnp.exp(scores - lse[..., None])
    low = soft.astype(BF16)
    grad_value = jnp.einsum("hqk,qhd->khd", low, grad_context, preferred_element_type=F32)
    grad_soft = jnp.einsum("qhd,khd->hqk", grad_context, value_rows, preferred_element_type=F32)
    inner = jnp.sum(soft * grad_soft, axis=-1, keepdims=True)
    grad_scores = (soft * (grad_soft - inner)).astype(BF16)
    scaling = HEAD_DIM ** (-0.5)
    grad_query = (
        jnp.einsum("hqk,khd->qhd", grad_scores, key_rows, preferred_element_type=F32) * scaling
    )
    grad_key = (
        jnp.einsum("hqk,qhd->khd", grad_scores, query_rows, preferred_element_type=F32) * scaling
    )
    return tuple((g.astype(BF16) for g in (grad_query, grad_key, grad_value)))


def local(
    tokens,
    cotangent,
    segment_ids,
    valid_count,
    qkv_weight,
    qv_bias,
    out_weight,
    out_bias,
    norm_gain,
    norm_shift,
    in_weight,
    in_bias,
    back_weight,
    back_bias,
    final_gain,
    final_shift,
):
    head_index = lax.axis_index("heads")
    devices = lax.axis_size("rows") * lax.axis_size("heads")
    token_count, width = tokens.shape
    row_length = segment_ids.shape[1]
    rows = token_count // row_length
    shard = qkv_weight.shape[0]
    small = [
        qv_bias[0],
        qv_bias[1],
        out_bias,
        norm_gain,
        norm_shift,
        in_bias,
        back_bias,
        final_gain,
        final_shift,
    ]
    sizes = [s.shape[0] for s in small]
    total = sum(sizes)
    lanes = -(-total // (shard * 128)) * 128
    packed = jnp.pad(jnp.concatenate(small), (0, shard * lanes - total)).reshape(shard, lanes)
    first = lax.all_gather(jnp.concatenate([qkv_weight, packed], axis=1), AXES, axis=0, tiled=True)
    qkv_all = first[:, : 3 * width]
    vectors = first[:, 3 * width :].reshape(devices, shard * lanes)
    parts = []
    at = 0
    for n in sizes:
        parts.append(vectors[:, at : at + n].reshape(devices * n).astype(F32))
        at += n
    q_bias, v_bias, out_bias_f, gain_f, shift_f, in_bias_f, back_bias_f, fgain_f, fshift_f = parts
    second = lax.all_gather(
        jnp.concatenate([out_weight, in_weight], axis=1), AXES, axis=0, tiled=True
    )
    out_all = second[:, :width]
    in_all = second[:, width:]
    back_all = lax.all_gather(back_weight, AXES, axis=0, tiled=True)
    segments = lax.dynamic_slice(segment_ids, (head_index * rows, 0), (rows, row_length))
    counts = lax.dynamic_slice(valid_count, (head_index * rows,), (rows,))
    bias_full = jnp.concatenate([q_bias, jnp.zeros_like(q_bias), v_bias])
    projected = (jnp.dot(tokens, qkv_all, preferred_element_type=F32) + bias_full).astype(BF16)
    heads = projected.reshape(rows, row_length, 3, HEADS, HEAD_DIM)
    contexts = [
        attend_forward(heads[r, :, 0], heads[r, :, 1], heads[r, :, 2], segments[r], counts[r])
        for r in range(rows)
    ]
    context = jnp.concatenate([c[0].reshape(row_length, width) for c in contexts], axis=0)
    valid = (jnp.arange(row_length)[None, :] < counts[:, None]).astype(F32).reshape(token_count, 1)
    attn = jnp.dot(context, out_all, preferred_element_type=F32) + out_bias_f
    hidden, n1, r1 = norm_forward(tokens.astype(F32) + attn, gain_f, shift_f)
    hidden_low = hidden.astype(BF16)
    preact = jnp.dot(hidden_low, in_all, preferred_element_type=F32) + in_bias_f
    cdf = 0.5 + 0.5 * lax.erf(preact * 0.5**0.5)
    activation = (preact * cdf).astype(BF16)
    slope = (
        cdf + preact * jnp.exp(-0.5 * preact * preact) * (1.0 / math.sqrt(2 * math.pi))
    ).astype(BF16)
    feed = jnp.dot(activation, back_all, preferred_element_type=F32) + back_bias_f
    finished, n2, r2 = norm_forward(hidden + feed, fgain_f, fshift_f)
    layer_out = (finished * valid).astype(BF16)
    grad_final = cotangent.astype(F32) * valid
    g_res2, g_fgain, g_fshift = norm_backward(grad_final, n2, r2, fgain_f)
    g_ffn = g_res2.astype(BF16)
    g_back_bias = jnp.sum(g_ffn.astype(F32), axis=0)
    g_back = jnp.einsum("tf,td->fd", activation, g_ffn, preferred_element_type=F32).astype(BF16)
    g_back = lax.psum_scatter(g_back, AXES, scatter_dimension=0, tiled=True)
    g_act = jnp.einsum("td,fd->tf", g_ffn, back_all, preferred_element_type=F32)
    g_pre = (g_act * slope.astype(F32)).astype(BF16)
    g_in_bias = jnp.sum(g_pre.astype(F32), axis=0)
    g_in = jnp.einsum("td,tf->df", hidden_low, g_pre, preferred_element_type=F32).astype(BF16)
    g_hidden = g_res2 + jnp.einsum("tf,df->td", g_pre, in_all, preferred_element_type=F32)
    g_res1, g_gain, g_shift = norm_backward(g_hidden, n1, r1, gain_f)
    g_attn = g_res1.astype(BF16)
    g_out_bias = jnp.sum(g_attn.astype(F32), axis=0)
    g_out = jnp.einsum("tc,td->cd", context, g_attn, preferred_element_type=F32).astype(BF16)
    g_oi = lax.psum_scatter(
        jnp.concatenate([g_out, g_in], axis=1), AXES, scatter_dimension=0, tiled=True
    )
    g_context = jnp.einsum("td,cd->tc", g_attn, out_all, preferred_element_type=F32).astype(BF16)
    g_heads = g_context.reshape(rows, row_length, HEADS, HEAD_DIM)
    grads = [
        attend_backward(
            heads[r, :, 0],
            heads[r, :, 1],
            heads[r, :, 2],
            segments[r],
            counts[r],
            contexts[r][1],
            g_heads[r],
        )
        for r in range(rows)
    ]
    g_proj = jnp.concatenate(
        [jnp.concatenate([g.reshape(row_length, width) for g in row], axis=1) for row in grads],
        axis=0,
    )
    g_qkv = jnp.einsum("td,tc->dc", tokens, g_proj, preferred_element_type=F32).astype(BF16)
    sums = jnp.sum(g_proj.astype(F32), axis=0).reshape(3, width)
    g_small = [
        sums[0],
        sums[2],
        g_out_bias,
        g_gain,
        g_shift,
        g_in_bias,
        g_back_bias,
        g_fgain,
        g_fshift,
    ]
    g_packed = jnp.concatenate([g.reshape(devices, -1) for g in g_small], axis=1)
    g_packed = jnp.pad(g_packed, ((0, 0), (0, shard * lanes - total))).astype(BF16)
    g_last = lax.psum_scatter(
        jnp.concatenate([g_qkv, g_packed.reshape(devices * shard, lanes)], axis=1),
        AXES,
        scatter_dimension=0,
        tiled=True,
    )
    grad_tokens = g_res1 + jnp.einsum("tc,dc->td", g_proj, qkv_all, preferred_element_type=F32)
    mine = g_last[:, 3 * width :].reshape(shard * lanes).astype(F32)
    own = []
    at = 0
    for n in sizes:
        own.append(mine[at : at + n])
        at += n
    return (
        layer_out,
        grad_tokens,
        g_last[:, : 3 * width].astype(F32),
        jnp.stack([own[0], own[1]]),
        g_oi[:, :width].astype(F32),
        own[2],
        own[3],
        own[4],
        g_oi[:, width:].astype(F32),
        own[5],
        g_back.astype(F32),
        own[6],
        own[7],
        own[8],
    )


def solution(mesh):
    both = P(AXES, None)
    vec = P(AXES)
    in_specs = (
        both,
        both,
        P("rows", None),
        P("rows"),
        both,
        P(None, AXES),
        both,
        vec,
        vec,
        vec,
        both,
        vec,
        both,
        vec,
        vec,
        vec,
    )
    out_specs = (
        both,
        both,
        both,
        P(None, AXES),
        both,
        vec,
        vec,
        vec,
        both,
        vec,
        both,
        vec,
        vec,
        vec,
    )
    return jax.shard_map(local, mesh=mesh, in_specs=in_specs, out_specs=out_specs, check_vma=False)
```

profile of v0, /device:TPU:0, one launch (start us, length us, event | category | flops | bytes accessed | tf_op | source)
XLA Modules:
  0.0 740.3 jit_solution(17252090711581574381)
XLA Ops:
  8.0 4.8 concatenate.34
  12.8 1.6 pad_maximum_fusion.6
  14.4 1.6 pad_maximum_fusion.5
  19.6 1.7 copy.88
  21.3 1.6 copy.78
  23.5 54.4 %all-gather.4.cloned.1.call-done = bf16[768,2432]{1,0:T(8,128)(2,1)} async-done(((bf16[24,2432]{1,0:T(8,128)(2,1)}), bf16[768,2432]{1,0:T(8,128)(2,1)}) %all-gather.4.cloned.1.call-update) | async-done | bytes 3735568 | tf_op jit(solution)/shard_map/all_gather | solution.py:114
  79.2 9.0 %fusion.17 = bf16[1024,2304]{0,1:T(8,128)(2,1)} fusion(bf16[1024,768]{1,0:T(8,128)(2,1)} %param.16, f32[2304]{0:T(1024)S(1)} %pad_maximum_fusion.7, bf16[768,2432]{1,0:T(8,128)(2,1)} %all-gather.4.cloned.1.call-done), kind=kOutput, calls=%fused_computation.36 | convolution fusion | flops 3628597248 | bytes 9839616 | tf_op jit(solution)/shard_map/dot_general | solution.py:132
  88.2 8.8 %reshape.390 = bf16[2,512,3,12,64]{1,0,4,3,2:T(2,128)(2,1)} reshape(bf16[1024,2304]{0,1:T(8,128)(2,1)} %fusion.17) | data formatting | bytes 9437184 | tf_op jit(solution)/shard_map/reshape | solution.py:133
  97.1 12.6 %fusion.72 = (bf16[1,512,1,12,64]{1,0,4,3,2:T(2,128)(2,1)}, bf16[1,512,1,12,64]{1,0,4,3,2:T(2,128)(2,1)S(1)}, bf16[1,512,1,12,64]{1,0,4,3,2:T(2,128)(2,1)}, bf16...) fusion(bf16[2,512,3,12,64]{1,0,4,3,2:T(2,128)(2,1)} %reshape.390), kind=kLoop, calls=%fused_computation.152 | loop fusion | bytes 9437184 | tf_op jit(solution)/shard_map/slice | solution.py:135
  109.7 2.1 fusion.20
  111.8 2.6 fusion.6
  114.4 1.9 copy-done
  117.1 9.1 %fusion.19 = (f32[12,512]{1,0:T(8,128)S(1)}, f32[12,512,512]{1,2,0:T(8,128)}) fusion(pred[512,512]{0,1:T(8,128)(4,1)S(1)} %fusion.47, bf16[1,512,1,12,64]{1,0,4,3,2:T(2,128)(2,1)} %get-tuple-element.71, bf16[1,512,1,12,64]{1,0,4,3,2:T(2,128)(2,1)} %get-tuple-element.72), kind=kOutput, calls=%fused_computation.39 | convolution fusion | flops 412084224 | bytes 14442496 | tf_op jit(solution)/shard_map/qhd,khd->hqk/dot_general | solution.py:41
  126.2 7.3 fusion.5
  133.6 5.9 fusion.44
  139.5 4.5 fusion.45
  144.0 3.7 all-gather.6.cloned.1.call-done
  147.7 3.7 fusion.77
  153.1 11.3 %multiply_convert_fusion.3 = (bf16[1024,3072]{1,0:T(8,128)(2,1)}, f32[1024,3072]{1,0:T(8,128)}) fusion(f32[3072]{0:T(1024)S(1)} %reshape.412, bf16[768,3840]{1,0:T(8,128)(2,1)S(1)} %copy-done.31, f32[1024,768]{0,1:T(8,128)S(1)} %get-tuple-element.106, f32[768]{0:T(1024)S(1)} %reshape.411, f32[768]{0:T(1024)S(1)} %reshape.410, ...), kind=kOutput, calls=%fused_computation.13 | convolution fusion | flops 4854644736 | bytes 26767360 | tf_op jit(solution)/shard_map/dot_general | solution.py:143
  164.4 48.5 %all-gather.8.cloned.1.call-done = bf16[3072,768]{1,0:T(8,128)(2,1)} async-done(((bf16[96,768]{1,0:T(8,128)(2,1)}), bf16[3072,768]{1,0:T(8,128)(2,1)}) %all-gather.8.cloned.1.call-update) | async-done | bytes 4718608 | tf_op jit(solution)/shard_map/all_gather | solution.py:128
  212.9 9.4 %fusion.78 = (f32[1024]{0:T(1024)S(1)}, f32[1024,768]{0,1:T(8,128)S(1)}) fusion(f32[768]{0:T(1024)S(1)} %reshape.413, bf16[1024,3072]{1,0:T(8,128)(2,1)} %get-tuple-element.107, bf16[3072,768]{1,0:T(8,128)(2,1)} %all-gather.8.cloned.1.call-done, f32[768]{0:T(1024)S(1)} %reshape.411, f32[768]{0:T(1024)S(1)} %reshape.410, f32[1024]{0:T(1024)S(1)} %add_rsqrt_fusion.1, ...), kind=kOutput, calls=%fused_computation.158 | convolution fusion | flops 4837342208 | bytes 17323008 | tf_op jit(solution)/shard_map/dot_general | solution.py:149
  222.8 3.8 multiply_reduce_fusion.2
  226.6 2.0 fusion.70
  228.6 16.2 %fusion.79 = (bf16[3072]{0:T(1024)(128)(2,1)}, bf16[1024,3072]{1,0:T(8,128)(2,1)}) fusion(f32[1024,3072]{1,0:T(8,128)} %get-tuple-element.108, f32[3072]{0:T(1024)S(1)} %reshape.412, bf16[1024,768]{0,1:T(8,128)(2,1)S(1)} %get-tuple-element.65, bf16[3072,768]{1,0:T(8,128)(2,1)S(1)} %bitcast.142), kind=kOutput, calls=%fused_computation.159 | convolution fusion | flops 4875875328 | bytes 25184256 | tf_op jit(solution)/shard_map/td,fd->tf/dot_general | solution.py:158
  244.9 11.4 %multiply_reduce_fusion.3 = (bf16[768]{0:T(1024)(128)(2,1)}, f32[1024]{0:T(1024)S(1)}, f32[1024]{0:T(1024)S(1)}, bf16[768]{0:T(1024)(128)(2,1)}, f32[1024,768]{0,1:T(8,128)S(1)}) fusion(f32[1024,768]{0,1:T(8,128)S(1)} %copy-done.3, f32[1024]{0:T(1024)S(1)} %add_rsqrt_fusion.1, f32[1024]{0:T(1024)S(1)} %broadcast_multiply_fusion.5, f32[768]{0:T(1024)S(1)} %reshape.410, ...), kind=kOutput, calls=%fused_computation.47 | convolution fusion | flops 4846776320 | bytes 22066176 | tf_op jit(solution)/shard_map/tf,df->td/dot_general | solution.py:162
  256.3 1.7 convert_reduce_fusion
  258.0 3.6 convolution_convert_fusion.3
  261.7 4.0 fusion.38
  265.7 8.4 %multiply_reduce_fusion.1 = (f32[12,512]{1,0:T(8,128)S(1)}, f32[12,512,512]{1,2,0:T(8,128)}) fusion(f32[12,512]{1,0:T(8,128)S(1)} %log_add_fusion.1, f32[12,512,512]{1,2,0:T(8,128)S(1)} %bitcast.113, pred[512,512]{0,1:T(8,128)(4,1)S(1)} %fusion.47, bf16[512,12,64]{0,2,1:T(8,128)(2,1)S(1)} %bitcast.117, bf16[1,512,1,12,64]{1,0,4,3,2:T(2,128)(2,1)} %get-tuple-element.68), kind=kOutput, calls=%fused_computation.10 | convolution fusion | flops 418375680 | bytes 27049984 | tf_op jit(solution)/shard_map/qhd,khd->hqk/dot_general | solution.py:62
  274.1 10.3 %multiply_convert_fusion.1 = bf16[12,512,512]{1,2,0:T(8,128)(2,1)S(1)} fusion(f32[12,512,512]{1,2,0:T(8,128)} %get-tuple-element.115, f32[12,512]{1,0:T(8,128)S(1)} %get-tuple-element.114, f32[12,512]{1,0:T(8,128)S(1)} %log_add_fusion.1, f32[12,512,512]{1,2,0:T(8,128)} %get-tuple-element.104, pred[512,512]{0,1:T(8,128)(4,1)S(1)} %fusion.47), kind=kLoop, calls=%fused_computation.9 | loop fusion | flops 18874368 | bytes 31768576 | tf_op jit(solution)/shard_map/convert_element_type | solution.py:64
  284.4 2.0 multiply_convert_fusion.7
  287.6 3.2 fusion.41
  290.8 7.1 multiply_reduce_fusion
  297.9 7.1 multiply_convert_fusion
  305.0 2.0 multiply_convert_fusion.5
  310.4 28.5 %fusion.18 = bf16[768,2304]{0,1:T(8,128)(2,1)S(1)} fusion(bf16[1024,768]{1,0:T(8,128)(2,1)S(1)} %copy-done.21, bf16[512,768]{0,1:T(8,128)(2,1)S(1)} %bitcast.134, bf16[512,768]{0,1:T(8,128)(2,1)S(1)} %bitcast.125, bf16[512,768]{0,1:T(8,128)(2,1)S(1)} %bitcast.128, bf16[512,768]{0,1:T(8,128)(2,1)S(1)} %bitcast.132, bf16[512,768]{0,1:T(8,128)(2,1)S(1)} %bitcast.119, ...), kind=kOutput, calls=%fused_computation.38 | convolution fusion | flops 3653959680 | bytes 9830400 | tf_op jit(solution)/shard_map/td,tc->dc/dot_general | solution.py:188
  341.1 1.4 reshape.402
  342.4 1.4 reshape.399
  343.8 1.4 reshape.400
  345.1 1.4 reshape.403
  346.5 1.4 reshape.401
  349.2 1.4 reshape_squeeze.9
  351.8 1.5 concatenate.42
  353.4 1.4 pad.10
  354.8 1.7 reshape.406
  356.5 1.7 copy.97
  358.2 3.1 pad_maximum_fusion.1
  361.4 1.3 copy-done.23
  362.7 10.0 %convolution_convert_fusion = bf16[3072,768]{1,0:T(8,128)(2,1)} fusion(bf16[1024,3072]{1,0:T(8,128)(2,1)} %get-tuple-element.107, bf16[1024,768]{0,1:T(8,128)(2,1)S(1)} %copy-done.23), kind=kOutput, calls=%fused_computation.33 | convolution fusion | flops 4834197504 | bytes 12582912 | tf_op jit(solution)/shard_map/tf,td->fd/dot_general | solution.py:156
  372.8 5.0 convolution_convert_fusion.4
  377.8 2.6 copy.99
  380.4 8.5 %convolution_convert_fusion.1 = bf16[768,3072]{1,0:T(8,128)(2,1)S(1)} fusion(bf16[1024,3072]{1,0:T(8,128)(2,1)} %get-tuple-element.117, f32[1024,768]{0,1:T(8,128)S(1)} %copy-done.4, f32[768]{0:T(1024)S(1)} %copy-done.29, f32[768]{0:T(1024)S(1)} %reshape.410, f32[1024]{0:T(1024)S(1)} %copy-done.27, f32[1024]{0:T(1024)S(1)} %broadcast_multiply_fusion.5), kind=kOutput, calls=%fused_computation.34 | convolution fusion | flops 4838129664 | bytes 14170112 | tf_op jit(solution)/shard_map/td,tf->df/dot_general | solution.py:161
  388.9 2.9 pad_maximum_fusion
  391.9 1.4 copy-done.11
  393.3 1.6 copy.100
  394.8 8.3 %fusion.32 = f32[1024,768]{0,1:T(8,128)S(1)} fusion(f32[1024,768]{0,1:T(8,128)} %copy-done.15, bf16[768,2432]{1,0:T(8,128)(2,1)} %all-gather.4.cloned.1.call-done, bf16[512,768]{0,1:T(8,128)(2,1)} %bitcast.135, bf16[512,768]{0,1:T(8,128)(2,1)} %bitcast.126, bf16[512,768]{0,1:T(8,128)(2,1)} %bitcast.129, bf16[512,768]{0,1:T(8,128)(2,1)} %bitcast.130, ...), kind=kOutput, calls=%fused_computation.71 | convolution fusion | flops 3652976640 | bytes 14548992 | tf_op jit(solution)/shard_map/tc,dc->td/dot_general | solution.py:209
  403.2 2.4 copy.101
  405.5 94.7 %all-reduce.5.cloned.1.call-done = bf16[768,2432]{0,1:T(8,128)(2,1)} async-done(((bf16[768,2432]{0,1:T(8,128)(2,1)}), bf16[768,2432]{0,1:T(8,128)(2,1)}) %all-reduce.5.cloned.1.call-update) | async-done | bytes 3735568
  500.2 1.5 dynamic-slice_convert_fusion
  505.6 106.8 %reduce-scatter.6.cloned.1.call-done = bf16[96,768]{1,0:T(8,128)(2,1)} async-done(((bf16[3072,768]{1,0:T(8,128)(2,1)}), bf16[96,768]{1,0:T(8,128)(2,1)}) %reduce-scatter.6.cloned.1.call-update) | async-done | bytes 147472 | tf_op jit(solution)/shard_map/reduce_scatter | solution.py:157
  612.4 1.6 convert_element_type.316
  614.0 116.2 %reduce-scatter.4.cloned.1.call-done = bf16[24,3840]{1,0:T(8,128)(2,1)} async-done(((bf16[768,3840]{1,0:T(8,128)(2,1)}), bf16[24,3840]{1,0:T(8,128)(2,1)}) %reduce-scatter.4.cloned.1.call-update) | async-done | bytes 184336 | tf_op jit(solution)/shard_map/reduce_scatter | solution.py:167
  730.2 1.4 slice_convert_fusion.1
  731.6 1.6 slice_convert_fusion
  (155 shorter events, 22.3 us)
Async XLA Ops:
  7.2 14.1 %copy-start.20 = (bf16[1024,768]{1,0:T(8,128)(2,1)S(1)}, bf16[1024,768]{1,0:T(8,128)(2,1)}, u32[]{:S(2)}) copy-start(bf16[1024,768]{1,0:T(8,128)(2,1)} %param.16) | copy-start | bytes 4718596
  7.2 15.7 %copy-start.30 = (s32[4,512]{1,0:T(4,128)S(1)}, s32[4,512]{1,0:T(4,128)}, u32[]{:S(2)}) copy-start(s32[4,512]{1,0:T(4,128)} %param.18) | copy-start | bytes 24580
  7.2 70.7 %all-gather.4.cloned.1.call-start = ((), (), s32[]{:S(2)}) async-start(), calls=%async_computation.2 | async-start | bytes 3852288 | tf_op jit(solution)/shard_map/all_gather | solution.py:114
  14.4 133.3 %all-gather.6.cloned.1.call-start = ((), (), s32[]{:S(2)}) async-start(), calls=%async_computation.3 | async-start | bytes 6082560 | tf_op jit(solution)/shard_map/all_gather | solution.py:123
  16.1 196.8 %all-gather.8.cloned.1.call-start = ((), (), s32[]{:S(2)}) async-start(), calls=%async_computation.4 | async-start | bytes 4866048 | tf_op jit(solution)/shard_map/all_gather | solution.py:128
  16.8 483.4 %all-reduce.5.cloned.1.call-start = ((), (), s32[]{:S(2)}) async-start(), calls=%async_computation.7 | async-start | bytes 7471104
  109.6 2.2 copy-start.5
  109.6 2.2 copy-start.7
  111.8 4.5 copy-start
  116.8 96.1 %copy-start.28 = (f32[768]{0:T(1024)}, f32[768]{0:T(1024)S(1)}, u32[]{:S(2)}) copy-start(f32[768]{0:T(1024)S(1)} %reshape.411) | copy-start | bytes 9220
  117.0 16.5 %slice-start = ((s8[12582912]{0:T(1024)(128)(4,1)}), s8[4194304]{0:T(1024)(128)(4,1)S(1)}, s32[]{:S(2)}) async-start(s8[12582912]{0:T(1024)(128)(4,1)} %bitcast.108), calls=%async_computation.8 | async-start | bytes 8388608
  117.0 16.5 %slice-start.1 = ((s8[12582912]{0:T(1024)(128)(4,1)}), s8[4194304]{0:T(1024)(128)(4,1)S(1)}, s32[]{:S(2)}) async-start(s8[12582912]{0:T(1024)(128)(4,1)} %bitcast.108), calls=%async_computation.9 | async-start | bytes 8388608
  126.2 7.4 slice-start.2
  133.6 5.9 copy-start.1
  133.6 5.9 copy-start.14
  139.5 8.3 %copy-start.32 = (bf16[12,64,512]{2,1,0:T(8,128)(2,1)S(1)}, bf16[12,64,512]{2,1,0:T(8,128)(2,1)}, u32[]{:S(2)}) copy-start(bf16[12,64,512]{2,1,0:T(8,128)(2,1)} %fusion.44) | copy-start | bytes 2359300
  147.7 5.4 copy-start.31
  151.5 1.7 copy-start.2
  153.1 103.1 %copy-start.26 = (f32[1024]{0:T(1024)}, f32[1024]{0:T(1024)S(1)}, u32[]{:S(2)}) copy-start(f32[1024]{0:T(1024)S(1)} %add_rsqrt_fusion.1) | copy-start | bytes 12292
  222.3 6.2 slice-start.9
  222.8 5.8 slice-start.10
  228.6 16.3 %copy-start.22 = (bf16[1024,768]{0,1:T(8,128)(2,1)}, bf16[1024,768]{0,1:T(8,128)(2,1)S(1)}, u32[]{:S(2)}) copy-start(bf16[1024,768]{0,1:T(8,128)(2,1)S(1)} %get-tuple-element.65) | copy-start | bytes 4718596
  228.6 16.3 %copy-start.3 = (f32[1024,768]{0,1:T(8,128)S(1)}, f32[1024,768]{0,1:T(8,128)}, u32[]{:S(2)}) copy-start(f32[1024,768]{0,1:T(8,128)} %copy-done.2) | copy-start | bytes 9437188
  228.6 33.1 %slice-start.6 = ((s8[12582912]{0:T(1024)(128)(4,1)}), s8[4194304]{0:T(1024)(128)(4,1)S(1)}, s32[]{:S(2)}) async-start(s8[12582912]{0:T(1024)(128)(4,1)} %bitcast.112), calls=%async_computation.14 | async-start | bytes 8388608
  228.6 33.1 %slice-start.7 = ((s8[12582912]{0:T(1024)(128)(4,1)}), s8[4194304]{0:T(1024)(128)(4,1)S(1)}, s32[]{:S(2)}) async-start(s8[12582912]{0:T(1024)(128)(4,1)} %bitcast.112), calls=%async_computation.15 | async-start | bytes 8388608
  244.9 16.8 %slice-start.8 = ((s8[12582912]{0:T(1024)(128)(4,1)}), s8[4194304]{0:T(1024)(128)(4,1)S(1)}, s32[]{:S(2)}) async-start(s8[12582912]{0:T(1024)(128)(4,1)} %bitcast.112), calls=%async_computation.16 | async-start | bytes 8388608
  258.0 3.7 copy-start.15
  265.7 21.9 %slice-start.3 = ((s8[12582912]{0:T(1024)(128)(4,1)}), s8[4194304]{0:T(1024)(128)(4,1)S(1)}, s32[]{:S(2)}) async-start(s8[12582912]{0:T(1024)(128)(4,1)} %bitcast.110), calls=%async_computation.11 | async-start | bytes 8388608
  265.7 21.9 %slice-start.4 = ((s8[12582912]{0:T(1024)(128)(4,1)}), s8[4194304]{0:T(1024)(128)(4,1)S(1)}, s32[]{:S(2)}) async-start(s8[12582912]{0:T(1024)(128)(4,1)} %bitcast.110), calls=%async_computation.12 | async-start | bytes 8388608
  274.1 10.3 %copy-start.10 = (bf16[1,512,1,12,64]{1,0,4,3,2:T(2,128)(2,1)S(1)}, bf16[1,512,1,12,64]{1,0,4,3,2:T(2,128)(2,1)}, u32[]{:S(2)}) copy-start(bf16[1,512,1,12,64]{1,0,4,3,2:T(2,128)(2,1)} %get-tuple-element.72) | copy-start | bytes 2359300
  274.1 13.5 %slice-start.5 = ((s8[12582912]{0:T(1024)(128)(4,1)}), s8[4194304]{0:T(1024)(128)(4,1)S(1)}, s32[]{:S(2)}) async-start(s8[12582912]{0:T(1024)(128)(4,1)} %bitcast.110), calls=%async_computation.13 | async-start | bytes 8388608
  284.4 2.0 copy-start.9
  286.4 24.0 %copy-start.16 = (bf16[12,64,512]{2,1,0:T(8,128)(2,1)}, bf16[12,64,512]{2,1,0:T(8,128)(2,1)S(1)}, u32[]{:S(2)}) copy-start(bf16[12,64,512]{2,1,0:T(8,128)(2,1)S(1)} %multiply_convert_fusion.7) | copy-start | bytes 2359300
  287.6 22.9 %copy-start.17 = (bf16[12,64,512]{2,1,0:T(8,128)(2,1)}, bf16[12,64,512]{2,1,0:T(8,128)(2,1)S(1)}, u32[]{:S(2)}) copy-start(bf16[12,64,512]{2,1,0:T(8,128)(2,1)S(1)} %multiply_convert_fusion.8) | copy-start | bytes 2359300
  287.6 3.2 copy-start.13
  290.8 19.6 %copy-start.25 = (bf16[12,64,512]{2,1,0:T(8,128)(2,1)}, bf16[12,64,512]{2,1,0:T(8,128)(2,1)S(1)}, u32[]{:S(2)}) copy-start(bf16[12,64,512]{2,1,0:T(8,128)(2,1)S(1)} %fusion.41) | copy-start | bytes 2359300
  297.9 7.1 copy-start.8
  305.0 2.0 copy-start.6
  307.0 3.4 copy-start.18
  307.0 1.4 copy-start.24
  308.2 30.8 %copy-start.19 = (bf16[12,64,512]{2,1,0:T(8,128)(2,1)}, bf16[12,64,512]{2,1,0:T(8,128)(2,1)S(1)}, u32[]{:S(2)}) copy-start(bf16[12,64,512]{2,1,0:T(8,128)(2,1)S(1)} %multiply_convert_fusion.6) | copy-start | bytes 2359300
  308.2 2.2 copy-start.21
  361.3 1.4 copy-start.23
  361.3 251.0 %reduce-scatter.6.cloned.1.call-start = ((), (), s32[]{:S(2)}) async-start(), calls=%async_computation.6 | async-start | bytes 4866048 | tf_op jit(solution)/shard_map/reduce_scatter | solution.py:157
  372.7 7.7 %copy-start.4 = (f32[1024,768]{0,1:T(8,128)S(1)}, f32[1024,768]{0,1:T(8,128)}, u32[]{:S(2)}) copy-start(f32[1024,768]{0,1:T(8,128)} %copy-done.2) | copy-start | bytes 9437188
  372.7 7.7 %copy-start.27 = (f32[1024]{0:T(1024)S(1)}, f32[1024]{0:T(1024)}, u32[]{:S(2)}) copy-start(f32[1024]{0:T(1024)} %copy-done.26) | copy-start | bytes 12292
  372.7 7.7 %copy-start.29 = (f32[768]{0:T(1024)S(1)}, f32[768]{0:T(1024)}, u32[]{:S(2)}) copy-start(f32[768]{0:T(1024)} %copy-done.28) | copy-start | bytes 9220
  372.7 357.5 %reduce-scatter.4.cloned.1.call-start = ((), (), s32[]{:S(2)}) async-start(), calls=%async_computation.5 | async-start | bytes 6082560 | tf_op jit(solution)/shard_map/reduce_scatter | solution.py:167
  380.4 8.5 %copy-start.12 = (bf16[768,768]{1,0:T(8,128)(2,1)S(1)}, bf16[768,768]{1,0:T(8,128)(2,1)}, u32[]{:S(2)}) copy-start(bf16[768,768]{1,0:T(8,128)(2,1)} %copy.99) | copy-start | bytes 3538948
  391.8 1.4 copy-start.11
Sparse Core Ops, SparseCore 0:
  14.5 63.3 all-gather.3
  81.3 66.3 all-gather.5
  150.6 62.2 all-gather.7
  361.5 138.7 all-reduce.4
  505.6 106.7 reduce-scatter.5
  617.9 112.3 reduce-scatter.3
where the time goes:
time: 748 us; the launch traced here: 740 us
  waiting for transfers between devices  425 us (57%)
  matrix products  176 us (24%)
  local copies, waits for them, and re-layouts  68.1 us (9%)
  other arithmetic  56.3 us (8%)
  between operations  15.1 us (2%)
    reduce_scatter x1, waiting for transfers between devices, local(): lax.psum_scatter(jnp.concatenate([g_out, g_in], axis=1), AXES, scatter_di...  116 us
    reduce_scatter x1, waiting for transfers between devices, local(): g_back = lax.psum_scatter(g_back, AXES, scatter_dimension=0, tiled=True)  107 us
    unnamed x7, waiting for transfers between devices  95.5 us
    all_gather x1, waiting for transfers between devices, local(): lax.all_gather(jnp.concatenate([qkv_weight, packed], axis=1), AXES, axis=...  54.4 us
    all_gather x1, waiting for transfers between devices, local(): back_all = lax.all_gather(back_weight, AXES, axis=0, tiled=True)  48.5 us
    dot_general x1, matrix products, local(): jnp.einsum('td,tc->dc', tokens, g_proj, preferred_element_type=F32)  28.5 us
    convert_element_type x2, other arithmetic, attend_backward(): grad_scores = (soft * (grad_soft - inner)).astype(BF16)  17.4 us
    dot_general x1, matrix products, local(): g_act = jnp.einsum('td,fd->tf', g_ffn, back_all, preferred_element_type=F32)  16.2 us
  transfers between devices with their start and end apart: 6, of which 6 were waited for; matrix products, arithmetic and copies ran while one was open for 18% of the time, Pallas kernels for 0%

commit v1 on v0

--- a/solution.py
+++ b/solution.py
@@ -10,6 +10,27 @@
 AXES = ("rows", "heads")
 F32 = jnp.float32
 BF16 = jnp.bfloat16
+
+
+def _touch_racks(row_data, d_out):
+    current_value = list(row_data.shape[1:])
+    current_value[d_out] *= row_data.shape[0]
+    return jnp.moveaxis(row_data, 0, d_out).reshape(current_value)
+
+
+def map_lanes(z_in, lane_axis):
+    count_all = lax.axis_size(lane_axis)
+    formed = z_in[None]
+    for ix in range(count_all.bit_length() - 1):
+        value_now = 1 << ix
+        current_block = lax.ppermute(
+            formed, axis_name=lane_axis, perm=[(idx, idx ^ value_now) for idx in range(count_all)]
+        )
+        opened = jnp.stack([formed, current_block])
+        mid_arr = lax.axis_index(lane_axis)
+        newest = mid_arr >> ix & 1
+        formed = jnp.where(newest == 0, opened, opened[::-1]).reshape(-1, *z_in.shape)
+    return formed
 
 
 def norm_forward(values, gain_row, shift_row):
@@ -111,7 +132,12 @@
     total = sum(sizes)
     lanes = -(-total // (shard * 128)) * 128
     packed = jnp.pad(jnp.concatenate(small), (0, shard * lanes - total)).reshape(shard, lanes)
-    first = lax.all_gather(jnp.concatenate([qkv_weight, packed], axis=1), AXES, axis=0, tiled=True)
+
+    def scan_the_frame(field_in, arr, dimension_no=0):
+        all_rows = map_lanes(field_in, arr)
+        return _touch_racks(all_rows, dimension_no)
+
+    first = scan_the_frame(jnp.concatenate([qkv_weight, packed], axis=1), AXES)
     qkv_all = first[:, : 3 * width]
     vectors = first[:, 3 * width :].reshape(devices, shard * lanes)
     parts = []

time: 748 us -> 787 us (1.052)
  waiting for transfers between devices: 425 us -> 449 us
  starting transfers between devices: 0.24 us -> 12.9 us
    ppermute x0 -> x5, waiting for transfers between devices: none -> 130 us  [map_lanes(): lax.ppermute(formed, axis_name=lane_axis, perm=[(idx, idx ^ value_now) fo...]
    all_gather x1 -> x0, waiting for transfers between devices: 54.4 us -> none  [local(): lax.all_gather(jnp.concatenate([qkv_weight, packed], axis=1), AXES, axis=...]
    all_gather x1, waiting for transfers between devices: 48.5 us -> 0.01 us  [local(): back_all = lax.all_gather(back_weight, AXES, axis=0, tiled=True)]
    ppermute x0 -> x5, starting transfers between devices: none -> 12.7 us  [map_lanes(): lax.ppermute(formed, axis_name=lane_axis, perm=[(idx, idx ^ value_now) fo...]
    unnamed x95 -> x113, local copies, waits for them, and re-layouts: 14.7 us -> 21.2 us
    unnamed x7 -> x6, waiting for transfers between devices: 95.5 us -> 95.4 us
  transfers between devices with their start and end apart: 6 -> 10, of which waited for: 6 -> 8; matrix products, arithmetic and copies ran while one was open for 18% -> 18% of each run, Pallas kernels for 0% -> 0%
where the time goes in v1:
time: 787 us; the launch traced here: 779 us
  waiting for transfers between devices  449 us (57%)
  matrix products  173 us (22%)
  local copies, waits for them, and re-layouts  72.9 us (9%)
  other arithmetic  55.9 us (7%)
  between operations  14.9 us (2%)
  starting transfers between devices  12.9 us (2%)
    ppermute x5, waiting for transfers between devices, map_lanes(): lax.ppermute(formed, axis_name=lane_axis, perm=[(idx, idx ^ value_now) fo...  130 us
    reduce_scatter x1, waiting for transfers between devices, local(): lax.psum_scatter(jnp.concatenate([g_out, g_in], axis=1), AXES, scatter_di...  116 us
    reduce_scatter x1, waiting for transfers between devices, local(): g_back = lax.psum_scatter(g_back, AXES, scatter_dimension=0, tiled=True)  107 us
    unnamed x6, waiting for transfers between devices  95.4 us
    dot_general x1, matrix products, local(): jnp.einsum('td,tc->dc', tokens, g_proj, preferred_element_type=F32)  22.6 us
    unnamed x113, local copies, waits for them, and re-layouts  21.2 us
    dot_general x2, matrix products, attend_backward(): jnp.einsum('qhd,khd->hqk', grad_context, value_rows, preferred_element_ty...  18.3 us
    dot_general x1, matrix products, local(): g_act = jnp.einsum('td,fd->tf', g_ffn, back_all, preferred_element_type=F32)  16.3 us
  transfers between devices with their start and end apart: 10, of which 8 were waited for; matrix products, arithmetic and copies ran while one was open for 18% of the time, Pallas kernels for 0%

profile of v1, /device:TPU:0, one launch (start us, length us, event | category | flops | bytes accessed | tf_op | source)
XLA Modules:
  0.0 778.6 jit_solution(10830606625853384599)
XLA Ops:
  7.2 1.6 pad_maximum_fusion.10
  9.6 4.8 concatenate.34
  16.9 2.9 collective-permute-start.1
  19.8 6.8 collective-permute-done.1
  26.8 2.3 collective-permute-start.2
  29.1 9.1 %collective-permute-done.2 = bf16[4,24,2432]{2,1,0:T(8,128)(2,1)S(1)} collective-permute-done((bf16[4,24,2432]{2,1,0:T(8,128)(2,1)S(1)}, bf16[4,24,2432]{2,1,0:T(8,128)(2,1)S(1)}, u32[]{:S(2)}, u32[]{:S(2)}) %collective-permute-start.2) | collective-permute-done | bytes 466976 | tf_op jit(solution)/shard_map/ppermute | solution.py:26
  38.5 1.7 collective-permute-start.3
  40.2 28.0 %collective-permute-done.3 = bf16[8,24,2432]{2,1,0:T(8,128)(2,1)S(1)} collective-permute-done((bf16[8,24,2432]{2,1,0:T(8,128)(2,1)S(1)}, bf16[8,24,2432]{2,1,0:T(8,128)(2,1)S(1)}, u32[]{:S(2)}, u32[]{:S(2)}) %collective-permute-start.3) | collective-permute-done | bytes 933920 | tf_op jit(solution)/shard_map/ppermute | solution.py:26
  68.7 5.2 collective-permute-start.4
  74.2 1.6 copy.78
  75.9 1.7 copy.88
  81.5 85.1 %collective-permute-done.4 = bf16[16,24,2432]{2,1,0:T(8,128)(2,1)} collective-permute-done((bf16[16,24,2432]{2,1,0:T(8,128)(2,1)S(1)}, bf16[16,24,2432]{2,1,0:T(8,128)(2,1)}, u32[]{:S(2)}, u32[]{:S(2)}) %collective-permute-start.4) | collective-permute-done | bytes 1867808 | tf_op jit(solution)/shard_map/ppermute | solution.py:26
  166.6 1.9 pad_maximum_fusion.1
  169.2 1.8 copy-done.15
  171.4 8.2 %fusion.17 = bf16[1024,2304]{0,1:T(8,128)(2,1)} fusion(bf16[1024,768]{1,0:T(8,128)(2,1)S(1)} %copy-done.28, f32[2304]{0:T(1024)S(1)} %pad_maximum_fusion.12, bf16[768,2432]{1,0:T(8,128)(2,1)} %bitcast.137), kind=kOutput, calls=%fused_computation.37 | convolution fusion | flops 3628597248 | bytes 9839616 | tf_op jit(solution)/shard_map/dot_general | solution.py:158
  179.6 8.8 %reshape.406 = bf16[2,512,3,12,64]{1,0,4,3,2:T(2,128)(2,1)} reshape(bf16[1024,2304]{0,1:T(8,128)(2,1)} %fusion.17) | data formatting | bytes 9437184 | tf_op jit(solution)/shard_map/reshape | solution.py:159
  188.5 12.5 %fusion.76 = (bf16[1,512,1,12,64]{1,0,4,3,2:T(2,128)(2,1)}, bf16[1,512,1,12,64]{1,0,4,3,2:T(2,128)(2,1)}, bf16[1,512,1,12,64]{1,0,4,3,2:T(2,128)(2,1)}, bf16[1,5...) fusion(bf16[2,512,3,12,64]{1,0,4,3,2:T(2,128)(2,1)} %reshape.406), kind=kLoop, calls=%fused_computation.166 | loop fusion | bytes 9437184 | tf_op jit(solution)/shard_map/slice | solution.py:161
  201.0 2.1 fusion.19
  203.2 2.6 fusion.5
  205.8 1.9 copy-done
  208.4 8.8 %fusion.20 = (f32[12,512]{1,0:T(8,128)S(1)}, f32[12,512,512]{1,2,0:T(8,128)}) fusion(pred[512,512]{0,1:T(8,128)(4,1)S(1)} %copy-done.5, bf16[1,512,1,12,64]{1,0,4,3,2:T(2,128)(2,1)} %get-tuple-element.73, bf16[1,512,1,12,64]{1,0,4,3,2:T(2,128)(2,1)} %get-tuple-element.69), kind=kOutput, calls=%fused_computation.41 | convolution fusion | flops 412084224 | bytes 14442496 | tf_op jit(solution)/shard_map/qhd,khd->hqk/dot_general | solution.py:62
  217.2 7.3 fusion.6
  224.6 5.9 fusion.45
  230.4 4.5 fusion.44
  234.9 3.7 fusion.81
  240.3 11.1 %multiply_convert_fusion.3 = (bf16[1024,3072]{1,0:T(8,128)(2,1)}, f32[1024,3072]{1,0:T(8,128)}) fusion(f32[3072]{0:T(1024)S(1)} %reshape.428, bf16[768,3840]{1,0:T(8,128)(2,1)S(1)} %copy-done.39, f32[1024,768]{0,1:T(8,128)S(1)} %get-tuple-element.110, f32[768]{0:T(1024)S(1)} %reshape.427, f32[768]{0:T(1024)S(1)} %reshape.426, ...), kind=kOutput, calls=%fused_computation.13 | convolution fusion | flops 4854644736 | bytes 26767360 | tf_op jit(solution)/shard_map/dot_general | solution.py:169
  251.4 9.4 %fusion.82 = (f32[1024]{0:T(1024)S(1)}, f32[1024,768]{0,1:T(8,128)S(1)}) fusion(f32[768]{0:T(1024)S(1)} %reshape.429, bf16[1024,3072]{1,0:T(8,128)(2,1)} %get-tuple-element.111, bf16[3072,768]{1,0:T(8,128)(2,1)} %all-gather.5.cloned.1.call-done, f32[768]{0:T(1024)S(1)} %reshape.427, f32[768]{0:T(1024)S(1)} %reshape.426, f32[1024]{0:T(1024)S(1)} %add_rsqrt_fusion.1, ...), kind=kOutput, calls=%fused_computation.172 | convolution fusion | flops 4837342208 | bytes 17323008 | tf_op jit(solution)/shard_map/dot_general | solution.py:175
  261.3 3.8 multiply_reduce_fusion.2
  265.1 2.0 fusion.74
  267.1 16.3 %fusion.83 = (bf16[3072]{0:T(1024)(128)(2,1)}, bf16[1024,3072]{1,0:T(8,128)(2,1)}) fusion(f32[1024,3072]{1,0:T(8,128)} %get-tuple-element.112, f32[3072]{0:T(1024)S(1)} %reshape.428, bf16[1024,768]{0,1:T(8,128)(2,1)S(1)} %get-tuple-element.65, bf16[3072,768]{1,0:T(8,128)(2,1)S(1)} %bitcast.175), kind=kOutput, calls=%fused_computation.173 | convolution fusion | flops 4875875328 | bytes 25184256 | tf_op jit(solution)/shard_map/td,fd->tf/dot_general | solution.py:184
  283.4 11.4 %multiply_reduce_fusion.3 = (bf16[768]{0:T(1024)(128)(2,1)}, f32[1024]{0:T(1024)S(1)}, f32[1024]{0:T(1024)S(1)}, bf16[768]{0:T(1024)(128)(2,1)}, f32[1024,768]{0,1:T(8,128)S(1)}) fusion(f32[1024,768]{0,1:T(8,128)S(1)} %copy-done.3, f32[1024]{0:T(1024)S(1)} %add_rsqrt_fusion.1, f32[1024]{0:T(1024)S(1)} %broadcast_multiply_fusion.5, f32[768]{0:T(1024)S(1)} %reshape.426, ...), kind=kOutput, calls=%fused_computation.49 | convolution fusion | flops 4846776320 | bytes 22066176 | tf_op jit(solution)/shard_map/tf,df->td/dot_general | solution.py:188
  294.8 1.7 convert_reduce_fusion
  296.5 1.7 copy-done.21
  298.2 2.8 convolution_convert_fusion.3
  301.2 7.1 multiply_reduce_fusion.1
  308.3 7.5 multiply_convert_fusion.1
  315.8 2.0 multiply_convert_fusion.8
  317.8 2.9 multiply_convert_fusion.7
  320.8 3.9 fusion.38
  324.7 11.2 %multiply_reduce_fusion = (f32[12,512]{1,0:T(8,128)S(1)}, f32[12,512,512]{1,2,0:T(8,128)}) fusion(f32[12,512]{1,0:T(8,128)S(1)} %log_add_fusion, f32[12,512,512]{1,2,0:T(8,128)} %get-tuple-element.106, pred[512,512]{0,1:T(8,128)(4,1)S(1)} %copy-done.5, bf16[512,12,64]{0,2,1:T(8,128)(2,1)S(1)} %bitcast.141, bf16[1,512,1,12,64]{1,0,4,3,2:T(2,128)(2,1)S(1)} %copy-done.17), kind=kOutput, calls=%fused_computation.7 | convolution fusion | flops 418375680 | bytes 27049984 | tf_op jit(solution)/shard_map/qhd,khd->hqk/dot_general | solution.py:83
  337.3 7.1 multiply_convert_fusion
  344.5 2.0 multiply_convert_fusion.6
  346.5 2.0 multiply_convert_fusion.5
  348.5 3.2 fusion.41
  352.2 22.6 %fusion.18 = bf16[768,2304]{0,1:T(8,128)(2,1)S(1)} fusion(bf16[1024,768]{1,0:T(8,128)(2,1)S(1)} %copy-done.29, bf16[512,768]{0,1:T(8,128)(2,1)S(1)} %bitcast.164, bf16[512,768]{0,1:T(8,128)(2,1)} %bitcast.155, bf16[512,768]{0,1:T(8,128)(2,1)S(1)} %bitcast.153, bf16[512,768]{0,1:T(8,128)(2,1)S(1)} %bitcast.161, bf16[512,768]{0,1:T(8,128)(2,1)S(1)} %bitcast.149, ...), kind=kOutput, calls=%fused_computation.39 | convolution fusion | flops 3653959680 | bytes 9830400 | tf_op jit(solution)/shard_map/td,tc->dc/dot_general | solution.py:214
  387.6 1.5 concatenate.42
  390.5 1.7 reshape.422
  392.2 1.7 copy.97
  394.0 3.1 pad_maximum_fusion.2
  398.5 9.8 %convolution_convert_fusion = bf16[3072,768]{1,0:T(8,128)(2,1)} fusion(bf16[1024,3072]{1,0:T(8,128)(2,1)} %get-tuple-element.111, bf16[1024,768]{0,1:T(8,128)(2,1)S(1)} %copy-done.31), kind=kOutput, calls=%fused_computation.34 | convolution fusion | flops 4834197504 | bytes 12582912 | tf_op jit(solution)/shard_map/tf,td->fd/dot_general | solution.py:182
  408.4 5.1 convolution_convert_fusion.4
  413.4 2.4 copy.99
  415.9 8.6 %convolution_convert_fusion.1 = bf16[768,3072]{1,0:T(8,128)(2,1)S(1)} fusion(bf16[1024,3072]{1,0:T(8,128)(2,1)} %get-tuple-element.121, f32[1024,768]{0,1:T(8,128)S(1)} %copy-done.4, f32[768]{0:T(1024)S(1)} %copy-done.37, f32[768]{0:T(1024)S(1)} %reshape.426, f32[1024]{0:T(1024)S(1)} %copy-done.35, f32[1024]{0:T(1024)S(1)} %broadcast_multiply_fusion.5), kind=kOutput, calls=%fused_computation.35 | convolution fusion | flops 4838129664 | bytes 14170112 | tf_op jit(solution)/shard_map/td,tf->df/dot_general | solution.py:187
  424.5 2.9 pad_maximum_fusion
  427.5 1.9 copy-done.22
  429.4 8.8 %fusion.32 = f32[1024,768]{0,1:T(8,128)} fusion(f32[1024,768]{0,1:T(8,128)S(1)} %copy-done.22, bf16[768,2432]{1,0:T(8,128)(2,1)} %bitcast.138, bf16[512,768]{0,1:T(8,128)(2,1)} %bitcast.165, bf16[512,768]{0,1:T(8,128)(2,1)} %bitcast.156, bf16[512,768]{0,1:T(8,128)(2,1)} %bitcast.151, bf16[512,768]{0,1:T(8,128)(2,1)} %bitcast.160, ...), kind=kOutput, calls=%fused_computation.75 | convolution fusion | flops 3652976640 | bytes 14548992 | tf_op jit(solution)/shard_map/tc,dc->td/dot_general | solution.py:235
  438.2 3.7 copy.101
  441.9 1.6 copy.100
  443.5 95.3 %all-reduce.5.cloned.1.call-done = bf16[768,2432]{0,1:T(8,128)(2,1)} async-done(((bf16[768,2432]{0,1:T(8,128)(2,1)}), bf16[768,2432]{0,1:T(8,128)(2,1)}) %all-reduce.5.cloned.1.call-update) | async-done | bytes 3735568
  539.8 1.5 dynamic-slice_convert_fusion
  544.1 106.9 %reduce-scatter.6.cloned.1.call-done = bf16[96,768]{1,0:T(8,128)(2,1)} async-done(((bf16[3072,768]{1,0:T(8,128)(2,1)}), bf16[96,768]{1,0:T(8,128)(2,1)}) %reduce-scatter.6.cloned.1.call-update) | async-done | bytes 147472 | tf_op jit(solution)/shard_map/reduce_scatter | solution.py:183
  651.0 1.6 convert_element_type.316
  652.6 116.2 %reduce-scatter.4.cloned.1.call-done = bf16[24,3840]{1,0:T(8,128)(2,1)} async-done(((bf16[768,3840]{1,0:T(8,128)(2,1)}), bf16[24,3840]{1,0:T(8,128)(2,1)}) %reduce-scatter.4.cloned.1.call-update) | async-done | bytes 184336 | tf_op jit(solution)/shard_map/reduce_scatter | solution.py:193
  768.8 1.6 slice_convert_fusion
  (190 shorter events, 35.0 us)
Async XLA Ops:
  7.2 227.7 %all-gather.3.cloned.1.call-start = ((), (), s32[]{:S(2)}) async-start(), calls=%async_computation.2 | async-start | bytes 6082560 | tf_op jit(solution)/shard_map/all_gather | solution.py:149
  8.8 242.6 %all-gather.5.cloned.1.call-start = ((), (), s32[]{:S(2)}) async-start(), calls=%async_computation.3 | async-start | bytes 4866048 | tf_op jit(solution)/shard_map/all_gather | solution.py:154
  15.3 1.5 collective-permute-start
  16.9 9.7 %collective-permute-start.1 = (bf16[2,24,2432]{2,1,0:T(8,128)(2,1)S(1)}, bf16[2,24,2432]{2,1,0:T(8,128)(2,1)S(1)}, u32[]{:S(2)}, u32[]{:S(2)}) collective-permute-start(bf16[2,24,2432]{2,1,0:T(8,128)(2,1)S(1)} %get-tuple-element.78), channel_id=1, source_target_pairs={{0,2},{1,3},{2,0},{3,1},{4,6},{5,7},{6,4},{7,5},{8,10},{9,11},{10,... | collective-permute-start | bytes 700424 | tf_op jit(solution)/shard_map/ppermute | solution.py:26
  26.8 11.4 %collective-permute-start.2 = (bf16[4,24,2432]{2,1,0:T(8,128)(2,1)S(1)}, bf16[4,24,2432]{2,1,0:T(8,128)(2,1)S(1)}, u32[]{:S(2)}, u32[]{:S(2)}) collective-permute-start(bf16[4,24,2432]{2,1,0:T(8,128)(2,1)S(1)} %bitcast.157), channel_id=1, source_target_pairs={{0,4},{1,5},{2,6},{3,7},{4,0},{5,1},{6,2},{7,3},{8,12},{9,13},{10,... | collective-permute-start | bytes 1400840 | tf_op jit(solution)/shard_map/ppermute | solution.py:26
  38.5 29.7 %collective-permute-start.3 = (bf16[8,24,2432]{2,1,0:T(8,128)(2,1)S(1)}, bf16[8,24,2432]{2,1,0:T(8,128)(2,1)S(1)}, u32[]{:S(2)}, u32[]{:S(2)}) collective-permute-start(bf16[8,24,2432]{2,1,0:T(8,128)(2,1)S(1)} %bitcast.139), channel_id=1, source_target_pairs={{0,8},{1,9},{2,10},{3,11},{4,12},{5,13},{6,14},{7,15},{8,0},{9,1},... | collective-permute-start | bytes 2801672 | tf_op jit(solution)/shard_map/ppermute | solution.py:26
  68.2 5.9 copy-start.40
  68.4 5.8 copy-start.27
  68.7 10.8 %copy-start.38 = (s32[4,512]{1,0:T(4,128)S(1)}, s32[4,512]{1,0:T(4,128)}, u32[]{:S(2)}) copy-start(s32[4,512]{1,0:T(4,128)} %param.18) | copy-start | bytes 24580
  68.7 97.8 %collective-permute-start.4 = (bf16[16,24,2432]{2,1,0:T(8,128)(2,1)S(1)}, bf16[16,24,2432]{2,1,0:T(8,128)(2,1)}, u32[]{:S(2)}, u32[]{:S(2)}) collective-permute-start(bf16[16,24,2432]{2,1,0:T(8,128)(2,1)S(1)} %bitcast.134), channel_id=1, source_target_pairs={{0,16},{1,17},{2,18},{3,19},{4,20},{5,21},{6,22},{7,23},{8,24},{9,... | collective-permute-start | bytes 5603336 | tf_op jit(solution)/shard_map/ppermute | solution.py:26
  74.0 464.8 %all-reduce.5.cloned.1.call-start = ((), (), s32[]{:S(2)}) async-start(), calls=%async_computation.6 | async-start | bytes 7471104
  168.5 2.9 copy-start.28
  169.2 1.8 copy-start.15
  188.5 12.6 %copy-start.6 = (pred[512,512]{0,1:T(8,128)(4,1)S(1)}, pred[512,512]{0,1:T(8,128)(4,1)}, u32[]{:S(2)}) copy-start(pred[512,512]{0,1:T(8,128)(4,1)} %fusion.47) | copy-start | bytes 786436
  201.0 2.2 copy-start.9
  201.0 2.2 copy-start.11
  203.2 4.5 copy-start
  203.2 5.2 copy-start.5
  208.1 43.3 %copy-start.36 = (f32[768]{0:T(1024)}, f32[768]{0:T(1024)S(1)}, u32[]{:S(2)}) copy-start(f32[768]{0:T(1024)S(1)} %reshape.427) | copy-start | bytes 9220
  208.4 16.1 %slice-start = ((s8[12582912]{0:T(1024)(128)(4,1)}), s8[4194304]{0:T(1024)(128)(4,1)S(1)}, s32[]{:S(2)}) async-start(s8[12582912]{0:T(1024)(128)(4,1)} %bitcast.128), calls=%async_computation.7 | async-start | bytes 8388608
  208.4 16.1 %slice-start.1 = ((s8[12582912]{0:T(1024)(128)(4,1)}), s8[4194304]{0:T(1024)(128)(4,1)S(1)}, s32[]{:S(2)}) async-start(s8[12582912]{0:T(1024)(128)(4,1)} %bitcast.128), calls=%async_computation.8 | async-start | bytes 8388608
  217.2 7.3 slice-start.2
  224.5 5.9 copy-start.1
  224.6 5.9 copy-start.16
  230.4 4.5 copy-start.41
  234.9 5.4 copy-start.39
  238.7 1.7 copy-start.2
  240.3 54.5 %copy-start.34 = (f32[1024]{0:T(1024)}, f32[1024]{0:T(1024)S(1)}, u32[]{:S(2)}) copy-start(f32[1024]{0:T(1024)S(1)} %add_rsqrt_fusion.1) | copy-start | bytes 12292
  260.9 6.2 slice-start.9
  261.3 5.8 slice-start.10
  267.1 16.3 %copy-start.30 = (bf16[1024,768]{0,1:T(8,128)(2,1)}, bf16[1024,768]{0,1:T(8,128)(2,1)S(1)}, u32[]{:S(2)}) copy-start(bf16[1024,768]{0,1:T(8,128)(2,1)S(1)} %get-tuple-element.65) | copy-start | bytes 4718596
  267.1 16.3 %copy-start.3 = (f32[1024,768]{0,1:T(8,128)S(1)}, f32[1024,768]{0,1:T(8,128)}, u32[]{:S(2)}) copy-start(f32[1024,768]{0,1:T(8,128)} %copy-done.2) | copy-start | bytes 9437188
  267.1 34.0 %slice-start.3 = ((s8[12582912]{0:T(1024)(128)(4,1)}), s8[4194304]{0:T(1024)(128)(4,1)S(1)}, s32[]{:S(2)}) async-start(s8[12582912]{0:T(1024)(128)(4,1)} %bitcast.130), calls=%async_computation.10 | async-start | bytes 8388608
  267.1 34.0 %slice-start.4 = ((s8[12582912]{0:T(1024)(128)(4,1)}), s8[4194304]{0:T(1024)(128)(4,1)S(1)}, s32[]{:S(2)}) async-start(s8[12582912]{0:T(1024)(128)(4,1)} %bitcast.130), calls=%async_computation.11 | async-start | bytes 8388608
  283.4 17.8 %slice-start.5 = ((s8[12582912]{0:T(1024)(128)(4,1)}), s8[4194304]{0:T(1024)(128)(4,1)S(1)}, s32[]{:S(2)}) async-start(s8[12582912]{0:T(1024)(128)(4,1)} %bitcast.130), calls=%async_computation.12 | async-start | bytes 8388608
  296.5 1.7 copy-start.21
  298.2 3.0 copy-start.18
  301.1 7.2 copy-start.19
  308.3 7.5 copy-start.12
  315.8 2.0 copy-start.10
  317.8 2.9 copy-start.20
  320.8 3.9 copy-start.17
  324.7 11.2 %slice-start.6 = ((s8[12582912]{0:T(1024)(128)(4,1)}), s8[4194304]{0:T(1024)(128)(4,1)S(1)}, s32[]{:S(2)}) async-start(s8[12582912]{0:T(1024)(128)(4,1)} %bitcast.132), calls=%async_computation.13 | async-start | bytes 8388608
  324.7 11.2 %slice-start.7 = ((s8[12582912]{0:T(1024)(128)(4,1)}), s8[4194304]{0:T(1024)(128)(4,1)S(1)}, s32[]{:S(2)}) async-start(s8[12582912]{0:T(1024)(128)(4,1)} %bitcast.132), calls=%async_computation.14 | async-start | bytes 8388608
  324.7 12.6 %slice-start.8 = ((s8[12582912]{0:T(1024)(128)(4,1)}), s8[4194304]{0:T(1024)(128)(4,1)S(1)}, s32[]{:S(2)}) async-start(s8[12582912]{0:T(1024)(128)(4,1)} %bitcast.132), calls=%async_computation.15 | async-start | bytes 8388608
  337.3 7.1 copy-start.8
  344.4 2.0 copy-start.7
  348.5 3.3 copy-start.26
  348.5 3.3 copy-start.25
  348.5 3.7 copy-start.23
  348.5 3.7 copy-start.24
  348.5 3.7 copy-start.29
  348.5 3.7 copy-start.32
  351.7 23.1 %copy-start.33 = (bf16[12,64,512]{2,1,0:T(8,128)(2,1)}, bf16[12,64,512]{2,1,0:T(8,128)(2,1)S(1)}, u32[]{:S(2)}) copy-start(bf16[12,64,512]{2,1,0:T(8,128)(2,1)S(1)} %fusion.41) | copy-start | bytes 2359300
  397.1 1.4 copy-start.31
  397.1 253.9 %reduce-scatter.6.cloned.1.call-start = ((), (), s32[]{:S(2)}) async-start(), calls=%async_computation.5 | async-start | bytes 4866048 | tf_op jit(solution)/shard_map/reduce_scatter | solution.py:183
  408.3 7.6 copy-start.4
  408.3 7.6 copy-start.35
  408.3 7.5 copy-start.37
  408.3 360.5 %reduce-scatter.4.cloned.1.call-start = ((), (), s32[]{:S(2)}) async-start(), calls=%async_computation.4 | async-start | bytes 6082560 | tf_op jit(solution)/shard_map/reduce_scatter | solution.py:193
  415.9 8.6 %copy-start.14 = (bf16[768,768]{1,0:T(8,128)(2,1)S(1)}, bf16[768,768]{1,0:T(8,128)(2,1)}, u32[]{:S(2)}) copy-start(bf16[768,768]{1,0:T(8,128)(2,1)} %copy.99) | copy-start | bytes 3538948
  427.4 2.0 copy-start.22
  438.2 3.7 copy-start.13
Sparse Core Ops, SparseCore 0:
  11.5 120.5 all-gather.2
  135.0 76.7 all-gather.4
  397.2 141.5 all-reduce.4
  544.1 106.8 reduce-scatter.5
  656.5 112.2 reduce-scatter.3
